TPU v7x, 32 devices: a whole 2x2x4 slice. The times are simulated.
32 devices in a mesh: energy: 8 (over z, y), wire: 4 (over x, core).
Axes of the slice: x: 2, y: 2, z: 4, core: 2. Of those that a mesh axis runs over, the one named last changes fastest.
Arguments:
- green_ret: float32 [2, 8, 8, 128, 128], P(None, 'energy', 'wire'), may hold values from -0.375 to 0.375
- coupling: float32 [2, 8, 128, 128], P(None, 'wire'), may hold values from -0.375 to 0.375
- sigma_less_in: float32 [2, 8, 8, 4096], P(None, 'energy', 'wire'), may hold values from -3 to 3
- sigma_greater_in: float32 [2, 8, 8, 4096], P(None, 'energy', 'wire'), may hold values from -3 to 3
- screened_less: float32 [2, 8, 8, 4096], P(None, 'energy', 'wire'), may hold values from -6 to 6
- screened_greater: float32 [2, 8, 8, 4096], P(None, 'energy', 'wire'), may hold values from -6 to 6
- pattern: int32 [8, 4096], P('wire'), may hold values from 0 to 16383, as said below
- counts: int32 [8], P('wire'), may hold values from 1024 to 4096, as said below
Outputs:
- green_less: float32 [2, 8, 8, 128, 128], P(None, 'energy', 'wire')
- green_greater: float32 [2, 8, 8, 128, 128], P(None, 'energy', 'wire')
- sigma_less: float32 [2, 8, 8, 4096], P(None, 'energy', 'wire')
- sigma_greater: float32 [2, 8, 8, 4096], P(None, 'energy', 'wire')
Inputs may be any that keep to these rules, and one draw needn't show every extreme that they name: `pattern`: within each block the 4096 positions are distinct; positions 0 and 16383 both occur in some block. `counts`: some block has all 4096 slots live and some block only 1024.
All inputs are finite; a program needn't handle non-finite values.
Results may differ from a plain program's by a relative error of at most 0.00016.
Values sent between devices are 32-bit elements; how exact they have to be, the bound alone decides.
A program may use at most 64 MiB of HBM per device.

v0:
```python
import functools

import jax
import jax.numpy as jnp
from jax import lax
from jax.experimental import pallas as pl
from jax.experimental.pallas import tpu as pltpu
from jax.sharding import PartitionSpec as P

MESH = pl.DeviceIdType.MESH
F32 = jnp.float32
BF16 = jnp.bfloat16


def split(x):
    hi = x.astype(BF16)
    lo = (x - hi.astype(F32)).astype(BF16)
    return hi, lo


def dot_nn(a, b):
    return lax.dot_general(a, b, (((1,), (0,)), ((), ())), preferred_element_type=F32)


def dot_nt(a, b):
    return lax.dot_general(a, b, (((1,), (1,)), ((), ())), preferred_element_type=F32)


def dot3(dot, a, b):
    return dot(a[0], b[0]) + (dot(a[1], b[0]) + dot(a[0], b[1]))


def full_one(row):
    n = row.shape[1] // 2
    re, im = row[:, :n], row[:, n:]
    return jnp.concatenate(
        [jnp.concatenate([re, im], axis=1), jnp.concatenate([-im, re], axis=1)], axis=0
    )


def full(row):
    return full_one(row[0]), full_one(row[1])


def sandwich(row, square, state):
    n = row[0].shape[0]
    stacked = state.reshape(2 * n, 2 * n)
    right = dot3(dot_nt, split(stacked), square)
    hi, lo = split(right)
    wide = tuple(
        jnp.concatenate([full_one(x[:n]), full_one(x[n:])], axis=1) for x in (hi, lo)
    )
    out = dot3(dot_nn, row, wide)
    return out[:, : 2 * n], out[:, 2 * n :]


def kernel(
    n_energy, n_wire,
    g_hbm, c_hbm, sl_hbm, sg_hbm, wl_hbm, wg_hbm, pat_hbm, cnt_ref,
    gl_hbm, gg_hbm, ol_ref, og_ref,
    g, c, sl, sg, wl, wg, pat,
    acc, st, pin, lhs, send_w, recv_w, send_g, recv_g, send_s, recv_s,
    in_sem, out_sem, ring_send, ring_recv, sw_sem, rw_sem, sg_sem, rg_sem, ss_sem, rs_sem,
):
    e = lax.axis_index("energy")
    w = lax.axis_index("wire")
    blocks = g.shape[1]
    n = g.shape[2]
    slots = pat.shape[1]
    part = slots // n_energy
    rows = 4 * blocks

    barrier = pltpu.get_barrier_semaphore()

    def greet(d, carry):
        peer = lax.rem(e + d, n_energy)
        pl.semaphore_signal(barrier, inc=1, device_id={"energy": peer}, device_id_type=MESH)
        return carry

    lax.fori_loop(1, n_energy, greet, 0)

    @pl.when(w > 0)
    def _():
        pl.semaphore_signal(barrier, inc=1, device_id={"wire": w - 1}, device_id_type=MESH)

    @pl.when(w < n_wire - 1)
    def _():
        pl.semaphore_signal(barrier, inc=1, device_id={"wire": w + 1}, device_id_type=MESH)

    pairs = [(pat_hbm, pat), (sl_hbm, sl), (sg_hbm, sg), (wl_hbm, wl), (wg_hbm, wg),
             (g_hbm, g), (c_hbm, c)]
    loads = [pltpu.make_async_copy(s, d, in_sem.at[i]) for i, (s, d) in enumerate(pairs)]
    for copy in loads:
        copy.start()

    loads[3].wait()
    loads[4].wait()
    for t in range(n_energy):
        for p in range(2):
            for k, ref in enumerate((wl, wg)):
                for b in range(blocks):
                    row = p * 2 * blocks + k * blocks + b
                    send_w[t, row : row + 1, :] = ref[p, b : b + 1, t * part : (t + 1) * part]
    beside = jnp.where(w > 0, 1, 0) + jnp.where(w < n_wire - 1, 1, 0)
    pl.semaphore_wait(barrier, n_energy - 1 + beside)

    def to_peer(src, dst, s_sem, r_sem, peer):
        return pltpu.make_async_remote_copy(
            src_ref=src.at[peer], dst_ref=dst.at[e], send_sem=s_sem.at[peer],
            recv_sem=r_sem.at[e], device_id={"energy": peer}, device_id_type=MESH)

    def from_peer(src, dst, s_sem, r_sem, peer):
        return pltpu.make_async_remote_copy(
            src_ref=src.at[peer], dst_ref=dst.at[peer], send_sem=s_sem.at[peer],
            recv_sem=r_sem.at[peer], device_id={"energy": peer}, device_id_type=MESH)

    def start_w(d, carry):
        to_peer(send_w, recv_w, sw_sem, rw_sem, lax.rem(e + d, n_energy)).start()
        return carry

    lax.fori_loop(1, n_energy, start_w, 0)
    recv_w[e] = send_w[e]

    for i in range(3):
        loads[i].wait()
    chunk = min(slots, 1024)

    def places(b, off, size):
        p = pat[b : b + 1, pl.ds(off, size)]
        slot = lax.broadcasted_iota(jnp.int32, (1, size), 1) + off
        row = jnp.where(slot < cnt_ref[b], lax.shift_right_logical(p, 7), n)
        col = lax.bitwise_and(p, 127)
        down = lax.broadcasted_iota(jnp.int32, (n, size), 0)
        return down == row, down == col

    acc[...] = jnp.zeros_like(acc)

    def scatter(i, carry):
        off = pl.multiple_of(i * chunk, chunk)
        for b in range(blocks):
            row_is, col_is = places(b, off, chunk)
            hot = jnp.where(row_is, 1.0, 0.0).astype(BF16)
            his, los = [], []
            for ref in (sl, sg):
                for p in range(2):
                    v = ref[p, b : b + 1, pl.ds(off, chunk)]
                    hi = v.astype(BF16).astype(F32)
                    his.append(jnp.where(col_is, hi, 0.0).astype(BF16))
                    los.append(jnp.where(col_is, v - hi, 0.0).astype(BF16))
            acc[b] += dot_nt(hot, jnp.concatenate(his + los, axis=0))
        return carry

    lax.fori_loop(0, slots // chunk, scatter, 0)

    loads[5].wait()
    loads[6].wait()
    mults = []
    total = None
    through = None
    for b in range(blocks):
        g_row = split(jnp.concatenate([g[0, b], g[1, b]], axis=1))
        c_row = split(jnp.concatenate([c[0, b], c[1, b]], axis=1))
        mult = split(dot3(dot_nn, g_row, full(c_row)))
        dense = acc[b]
        dense = dense[:, : 4 * n] + dense[:, 4 * n :]
        source = sandwich(g_row, full(g_row), jnp.stack([dense[:, : 2 * n], dense[:, 2 * n :]]))
        if b == 0:
            through = mult
            total = source
        else:
            square = full(mult)
            moved = sandwich(mult, square, st[b - 1])
            total = (source[0] + moved[0], source[1] + moved[1])
            through = split(dot3(dot_nn, mult, full(through)))
        st[b, 0] = total[0]
        st[b, 1] = total[1]
        mults.append(through)

    last = blocks - 1

    def ring(k):
        return pltpu.make_async_remote_copy(
            src_ref=st.at[last, k], dst_ref=pin.at[k], send_sem=ring_send.at[k],
            recv_sem=ring_recv.at[k], device_id={"wire": w + 1}, device_id_type=MESH)

    def arrive(k):
        return pltpu.make_async_remote_copy(
            src_ref=st.at[last, k], dst_ref=pin.at[k], send_sem=ring_send.at[k],
            recv_sem=ring_recv.at[k], device_id={"wire": w - 1}, device_id_type=MESH)

    def advance(b):
        more = sandwich(mults[b], full(mults[b]), pin[...])
        st[b, 0] += more[0]
        st[b, 1] += more[1]

    @pl.when(w > 0)
    def _():
        arrive(0).wait_recv()
        arrive(1).wait_recv()
        advance(last)

    @pl.when(w < n_wire - 1)
    def _():
        ring(0).start()
        ring(1).start()

    @pl.when(w > 0)
    def _():
        for b in range(last):
            advance(b)

    outs = []
    for b in range(blocks):
        for k, dst in enumerate((gl_hbm, gg_hbm)):
            for p in range(2):
                outs.append(pltpu.make_async_copy(
                    st.at[b, k, :, pl.ds(p * n, n)], dst.at[p, b], out_sem.at[len(outs)]))
    for copy in outs:
        copy.start()

    for b in range(blocks):
        for k in range(2):
            hi, lo = split(st[b, k])
            for p in range(2):
                at = (2 * k + p) * n
                lhs[b, at : at + n, :n] = hi[:, p * n : (p + 1) * n]
                lhs[b, at : at + n, n:] = lo[:, p * n : (p + 1) * n]

    def gather(d, carry):
        t = lax.rem(e + d, n_energy)
        off = pl.multiple_of(t * part, part)
        for b in range(blocks):
            row_is, col_is = places(b, off, part)
            hot = jnp.where(col_is, 1.0, 0.0).astype(BF16)
            taken = dot_nn(lhs[b], jnp.concatenate([hot, hot], axis=0))
            for k in range(2):
                for p in range(2):
                    at = (2 * k + p) * n
                    row = p * 2 * blocks + k * blocks + b
                    picked = jnp.where(row_is, taken[at : at + n], 0.0)
                    send_g[t, row : row + 1, :] = jnp.sum(picked, axis=0, keepdims=True)

        @pl.when(d < n_energy)
        def _():
            to_peer(send_g, recv_g, sg_sem, rg_sem, t).start()

        return carry

    lax.fori_loop(1, n_energy + 1, gather, 0)
    recv_g[e] = send_g[e]

    def land(d, carry):
        peer = lax.rem(e + d, n_energy)
        from_peer(send_w, recv_w, sw_sem, rw_sem, peer).wait_recv()
        from_peer(send_g, recv_g, sg_sem, rg_sem, peer).wait_recv()
        return carry

    lax.fori_loop(1, n_energy, land, 0)

    half = rows // 2
    scale = n_energy ** -0.5
    plain, turned, straight, crossed = [], [], [], []
    for k in range(n_energy):
        x = recv_g[k]
        y = recv_w[k]
        plain.append(x)
        turned.append(jnp.concatenate([x[half:], x[:half]], axis=0))
        straight.append(jnp.concatenate([y[:half], y[:half]], axis=0))
        crossed.append(jnp.concatenate([-y[half:], y[half:]], axis=0))
    for f in range(n_energy):
        total = None
        for k in range(f + 1):
            term = plain[f - k] * straight[k] + turned[f - k] * crossed[k]
            total = term if total is None else total + term
        send_s[f] = jnp.concatenate([-scale * total[half:], scale * total[:half]], axis=0)

        @pl.when(e != f)
        def _():
            to_peer(send_s, recv_s, ss_sem, rs_sem, f).start()

    recv_s[e] = send_s[e]

    def land_s(d, carry):
        peer = lax.rem(e + d, n_energy)
        from_peer(send_s, recv_s, ss_sem, rs_sem, peer).wait_recv()
        return carry

    lax.fori_loop(1, n_energy, land_s, 0)
    for t in range(n_energy):
        for p in range(2):
            for k, ref in enumerate((ol_ref, og_ref)):
                for b in range(blocks):
                    row = p * 2 * blocks + k * blocks + b
                    ref[p, b : b + 1, t * part : (t + 1) * part] = recv_s[t, row : row + 1, :]

    def drain(d, carry):
        peer = lax.rem(e + d, n_energy)
        to_peer(send_w, recv_w, sw_sem, rw_sem, peer).wait_send()
        to_peer(send_g, recv_g, sg_sem, rg_sem, peer).wait_send()
        to_peer(send_s, recv_s, ss_sem, rs_sem, peer).wait_send()
        return carry

    lax.fori_loop(1, n_energy, drain, 0)

    @pl.when(w < n_wire - 1)
    def _():
        ring(0).wait_send()
        ring(1).wait_send()

    for copy in outs:
        copy.wait()


def on_device(n_energy, n_wire, green_ret, coupling, sl, sg, wl, wg, pattern, counts):
    blocks, n = green_ret.shape[2], green_ret.shape[3]
    slots = pattern.shape[1]
    part = slots // n_energy
    rows = 4 * blocks
    g = green_ret.reshape(2, blocks, n, n)
    vals = [x.reshape(2, blocks, slots) for x in (sl, sg, wl, wg)]
    any_spec = pl.BlockSpec(memory_space=pl.ANY)
    hbm_spec = pl.BlockSpec(memory_space=pltpu.HBM)
    vmem_spec = pl.BlockSpec(memory_space=pltpu.VMEM)
    dma = pltpu.SemaphoreType.DMA
    mail = pltpu.VMEM((n_energy, rows, part), F32)
    out = pl.pallas_call(
        functools.partial(kernel, n_energy, n_wire),
        out_shape=[
            jax.ShapeDtypeStruct((2, blocks, n, n), F32),
            jax.ShapeDtypeStruct((2, blocks, n, n), F32),
            jax.ShapeDtypeStruct((2, blocks, slots), F32),
            jax.ShapeDtypeStruct((2, blocks, slots), F32),
        ],
        in_specs=[hbm_spec] * 7 + [pl.BlockSpec(memory_space=pltpu.SMEM)],
        out_specs=[any_spec, any_spec, vmem_spec, vmem_spec],
        scratch_shapes=[
            pltpu.VMEM((2, blocks, n, n), F32),
            pltpu.VMEM((2, blocks, n, n), F32),
            pltpu.VMEM((2, blocks, slots), F32),
            pltpu.VMEM((2, blocks, slots), F32),
            pltpu.VMEM((2, blocks, slots), F32),
            pltpu.VMEM((2, blocks, slots), F32),
            pltpu.VMEM((blocks, slots), jnp.int32),
            pltpu.VMEM((blocks, n, 8 * n), F32),
            pltpu.VMEM((blocks, 2, n, 2 * n), F32),
            pltpu.VMEM((2, n, 2 * n), F32),
            pltpu.VMEM((blocks, 4 * n, 2 * n), BF16),
            mail, mail, mail, mail, mail, mail,
            dma((7,)), dma((4 * blocks,)), dma((2,)), dma((2,)),
            dma((n_energy,)), dma((n_energy,)), dma((n_energy,)),
            dma((n_energy,)), dma((n_energy,)), dma((n_energy,)),
        ],
        compiler_params=pltpu.CompilerParams(
            collective_id=0, has_side_effects=True, vmem_limit_bytes=40 * 1024 * 1024
        ),
    )(g, coupling, *vals, pattern, counts)
    return (
        out[0].reshape(green_ret.shape),
        out[1].reshape(green_ret.shape),
        out[2].reshape(sl.shape),
        out[3].reshape(sl.shape),
    )


def solution(mesh):
    blocks_spec = P(None, "energy", "wire", None, None)
    slots_spec = P(None, "energy", "wire", None)
    in_specs = (
        blocks_spec, P(None, "wire", None, None),
        slots_spec, slots_spec, slots_spec, slots_spec,
        P("wire", None), P("wire"),
    )
    out_specs = (blocks_spec, blocks_spec, slots_spec, slots_spec)
    return jax.shard_map(
        functools.partial(on_device, mesh.shape["energy"], mesh.shape["wire"]),
        mesh=mesh, in_specs=in_specs, out_specs=out_specs, check_vma=False,
    )
```

profile of v0, /device:TPU:3, one launch (start us, length us, event | category | flops | bytes accessed | tf_op | source)
XLA Modules:
  0.0 43.9 jit_solution(4608413428517033428)
XLA Ops:
  0.6 0.0 copy-start.7
  0.6 0.6 %copy-done.7 = s32[2]{0:T(128)S(1)} copy-done((s32[2]{0:T(128)S(1)}, s32[2]{0:T(128)}, u32[]{:S(2)}) %copy-start.7) | copy-done | bytes 32
  1.3 0.0 copy-start
  1.3 0.9 %copy-done = f32[2,1,2,128,128]{4,3,2,1,0:T(8,128)S(1)} copy-done((f32[2,1,2,128,128]{4,3,2,1,0:T(8,128)S(1)}, f32[2,1,2,128,128]{4,3,2,1,0:T(8,128)}, u32[]{:S(2)}) %copy-start) | copy-done | bytes 262168
  2.2 0.0 copy-start.1
  2.2 0.9 %copy-done.1 = f32[2,2,128,128]{3,2,1,0:T(8,128)S(1)} copy-done((f32[2,2,128,128]{3,2,1,0:T(8,128)S(1)}, f32[2,2,128,128]{3,2,1,0:T(8,128)}, u32[]{:S(2)}) %copy-start.1) | copy-done | bytes 262168
  3.2 0.0 copy-start.2
  3.2 0.8 %copy-done.2 = f32[2,1,2,4096]{3,2,1,0:T(2,128)S(1)} copy-done((f32[2,1,2,4096]{3,2,1,0:T(2,128)S(1)}, f32[2,1,2,4096]{3,2,1,0:T(2,128)}, u32[]{:S(2)}) %copy-start.2) | copy-done | bytes 65560
  4.0 0.0 copy-start.3
  4.0 0.8 %copy-done.3 = f32[2,1,2,4096]{3,2,1,0:T(2,128)S(1)} copy-done((f32[2,1,2,4096]{3,2,1,0:T(2,128)S(1)}, f32[2,1,2,4096]{3,2,1,0:T(2,128)}, u32[]{:S(2)}) %copy-start.3) | copy-done | bytes 65560
  4.9 0.0 copy-start.4
  4.9 0.8 %copy-done.4 = f32[2,1,2,4096]{3,2,1,0:T(2,128)S(1)} copy-done((f32[2,1,2,4096]{3,2,1,0:T(2,128)S(1)}, f32[2,1,2,4096]{3,2,1,0:T(2,128)}, u32[]{:S(2)}) %copy-start.4) | copy-done | bytes 65560
  5.7 0.0 copy-start.5
  5.7 0.8 %copy-done.5 = f32[2,1,2,4096]{3,2,1,0:T(2,128)S(1)} copy-done((f32[2,1,2,4096]{3,2,1,0:T(2,128)S(1)}, f32[2,1,2,4096]{3,2,1,0:T(2,128)}, u32[]{:S(2)}) %copy-start.5) | copy-done | bytes 65560
  6.6 0.0 copy-start.6
  6.6 0.8 %copy-done.6 = s32[2,4096]{1,0:T(2,128)S(1)} copy-done((s32[2,4096]{1,0:T(2,128)S(1)}, s32[2,4096]{1,0:T(2,128)}, u32[]{:S(2)}) %copy-start.6) | copy-done | bytes 32792
  7.3 33.9 %shard_map.111 = (f32[2,2,128,128]{3,2,1,0:T(8,128)S(1)}, f32[2,2,128,128]{3,2,1,0:T(8,128)S(1)}, f32[2,2,4096]{2,1,0:T(2,128)S(1)}, f32[2,2,4096]{2,1,0:T(2,128)S(1)}) custom-call(f32[2,2,128,128]{3,2,1,0:T(8,128)S(1)} %bitcast.19, f32[2,2,128,128]{3,2,1,0:T(8,128)S(1)} %copy-done.1, f32[2,2,4096]{2,1,0:T(2,128)S(1)} %bitcast.22, ...), custom_call_target="tpu_custom_call" | custom-call | tf_op jit(solution)/shard_map/pallas_call | solution.py:326
  41.2 0.7 %copy.20 = f32[2,1,2,128,128]{4,3,2,1,0:T(8,128)} copy(f32[2,1,2,128,128]{4,3,2,1,0:T(8,128)S(1)} %bitcast.18) | data formatting | bytes 524288
  41.9 0.7 %copy.21 = f32[2,1,2,128,128]{4,3,2,1,0:T(8,128)} copy(f32[2,1,2,128,128]{4,3,2,1,0:T(8,128)S(1)} %bitcast.17) | data formatting | bytes 524288
  42.6 0.6 %copy.22 = f32[2,1,2,4096]{3,2,1,0:T(2,128)} copy(f32[2,1,2,4096]{3,2,1,0:T(2,128)S(1)} %bitcast.21) | data formatting | bytes 131072
  43.3 0.6 %copy.23 = f32[2,1,2,4096]{3,2,1,0:T(2,128)} copy(f32[2,1,2,4096]{3,2,1,0:T(2,128)S(1)} %bitcast.20) | data formatting | bytes 131072
Async XLA Ops:
  0.6 0.7 %copy-start.7 = (s32[2]{0:T(128)S(1)}, s32[2]{0:T(128)}, u32[]{:S(2)}) copy-start(s32[2]{0:T(128)} %cnt_ref.1) | copy-start | bytes 28
  1.3 0.9 %copy-start = (f32[2,1,2,128,128]{4,3,2,1,0:T(8,128)S(1)}, f32[2,1,2,128,128]{4,3,2,1,0:T(8,128)}, u32[]{:S(2)}) copy-start(f32[2,1,2,128,128]{4,3,2,1,0:T(8,128)} %param.8) | copy-start | bytes 786436
  2.2 0.9 %copy-start.1 = (f32[2,2,128,128]{3,2,1,0:T(8,128)S(1)}, f32[2,2,128,128]{3,2,1,0:T(8,128)}, u32[]{:S(2)}) copy-start(f32[2,2,128,128]{3,2,1,0:T(8,128)} %c_hbm.1) | copy-start | bytes 786436
  3.2 0.8 %copy-start.2 = (f32[2,1,2,4096]{3,2,1,0:T(2,128)S(1)}, f32[2,1,2,4096]{3,2,1,0:T(2,128)}, u32[]{:S(2)}) copy-start(f32[2,1,2,4096]{3,2,1,0:T(2,128)} %param.10) | copy-start | bytes 196612
  4.0 0.8 %copy-start.3 = (f32[2,1,2,4096]{3,2,1,0:T(2,128)S(1)}, f32[2,1,2,4096]{3,2,1,0:T(2,128)}, u32[]{:S(2)}) copy-start(f32[2,1,2,4096]{3,2,1,0:T(2,128)} %param.11) | copy-start | bytes 196612
  4.9 0.8 %copy-start.4 = (f32[2,1,2,4096]{3,2,1,0:T(2,128)S(1)}, f32[2,1,2,4096]{3,2,1,0:T(2,128)}, u32[]{:S(2)}) copy-start(f32[2,1,2,4096]{3,2,1,0:T(2,128)} %param.12) | copy-start | bytes 196612
  5.7 0.8 %copy-start.5 = (f32[2,1,2,4096]{3,2,1,0:T(2,128)S(1)}, f32[2,1,2,4096]{3,2,1,0:T(2,128)}, u32[]{:S(2)}) copy-start(f32[2,1,2,4096]{3,2,1,0:T(2,128)} %param.13) | copy-start | bytes 196612
  6.6 0.8 %copy-start.6 = (s32[2,4096]{1,0:T(2,128)S(1)}, s32[2,4096]{1,0:T(2,128)}, u32[]{:S(2)}) copy-start(s32[2,4096]{1,0:T(2,128)} %pat_hbm.1) | copy-start | bytes 98308
where the time goes:
time: 44.3 us; the launch traced here: 43.9 us
  Pallas kernels  33.9 us (77%)
  local copies, waits for them, and re-layouts  9.33 us (21%)
  between operations  0.66 us (1%)
    pallas_call x1, Pallas kernels, on_device(): pl.pallas_call(functools.partial(kernel, n_energy, n_wire), out_shape=[ja...  33.9 us
    unnamed x20, local copies, waits for them, and re-layouts  9.33 us

commit v1 on v0

--- a/solution.py
+++ b/solution.py
@@ -308,6 +308,17 @@
         ring(1).wait_send()
 
     for copy in outs:
+        copy.wait()
+
+
+def hand_over(*refs):
+    count = (len(refs) - 1) // 2
+    copies = [
+        pltpu.make_async_copy(refs[i], refs[count + i], refs[-1].at[i]) for i in range(count)
+    ]
+    for copy in copies:
+        copy.start()
+    for copy in copies:
         copy.wait()
 
 
@@ -351,9 +362,17 @@
             dma((n_energy,)), dma((n_energy,)), dma((n_energy,)),
         ],
         compiler_params=pltpu.CompilerParams(
-            collective_id=0, has_side_effects=True, vmem_limit_bytes=40 * 1024 * 1024
+            collective_id=0, has_side_effects=True, vmem_limit_bytes=60 * 1024 * 1024
         ),
     )(g, coupling, *vals, pattern, counts)
+    out = pl.pallas_call(
+        hand_over,
+        out_shape=[jax.ShapeDtypeStruct(x.shape, x.dtype) for x in out],
+        in_specs=[hbm_spec] * 4,
+        out_specs=[hbm_spec] * 4,
+        scratch_shapes=[dma((4,))],
+        compiler_params=pltpu.CompilerParams(vmem_limit_bytes=60 * 1024 * 1024),
+    )(*out)
     return (
         out[0].reshape(green_ret.shape),
         out[1].reshape(green_ret.shape),

time: 44.3 us -> 56.4 us (1.27)
  Pallas kernels: 33.9 us -> 55.6 us
  local copies, waits for them, and re-layouts: 9.33 us -> 0 us
    pallas_call x0 -> x1, Pallas kernels: none -> 21 us  [on_device(): pl.pallas_call(hand_over, out_shape=[jax.ShapeDtypeStruct(x.shape, x.dtyp...]
    unnamed x20 -> x0, local copies, waits for them, and re-layouts: 9.33 us -> none
    pallas_call x1, Pallas kernels: 33.9 us -> 34.6 us  [on_device(): pl.pallas_call(functools.partial(kernel, n_energy, n_wire), out_shape=[ja...]
where the time goes in v1:
time: 56.4 us; the launch traced here: 56.3 us
  Pallas kernels  55.6 us (99%)
  between operations  0.64 us (1%)
    pallas_call x1, Pallas kernels, on_device(): pl.pallas_call(functools.partial(kernel, n_energy, n_wire), out_shape=[ja...  34.6 us
    pallas_call x1, Pallas kernels, on_device(): pl.pallas_call(hand_over, out_shape=[jax.ShapeDtypeStruct(x.shape, x.dtyp...  21 us

profile of v1, /device:TPU:3, one launch (start us, length us, event | category | flops | bytes accessed | tf_op | source)
XLA Modules:
  0.0 56.3 jit_solution(12424050885543514041)
XLA Ops:
  0.6 34.6 %shard_map.111 = (f32[2,2,128,128]{3,2,1,0:T(8,128)}, f32[2,2,128,128]{3,2,1,0:T(8,128)}, f32[2,2,4096]{2,1,0:T(2,128)}, f32[2,2,4096]{2,1,0:T(2,128)}) custom-call(f32[2,2,128,128]{3,2,1,0:T(8,128)} %bitcast.17, f32[2,2,128,128]{3,2,1,0:T(8,128)} %c_hbm.1, f32[2,2,4096]{2,1,0:T(2,128)} %bitcast.18, f32[2,2,4096]{2,1,0:T(2,128)} %bitcast.19, ...), custom_call_target="tpu_custom_call" | custom-call | tf_op jit(solution)/shard_map/pallas_call | solution.py:337
  35.3 21.0 %shard_map.112 = (f32[2,2,128,128]{3,2,1,0:T(8,128)}, f32[2,2,128,128]{3,2,1,0:T(8,128)}, f32[2,2,4096]{2,1,0:T(2,128)}, f32[2,2,4096]{2,1,0:T(2,128)}) custom-call(f32[2,2,128,128]{3,2,1,0:T(8,128)} %get-tuple-element.12.refs_0_, f32[2,2,128,128]{3,2,1,0:T(8,128)} %get-tuple-element.13.refs_1_, f32[2,2,4096]{2,1,0:T(2,128)} %get-tuple-element.14.refs_2_, ...), custom_call_target="tpu_custom_call" | custom-call | tf_op jit(solution)/shard_map/pallas_call | solution.py:368

commit v2 on v0

--- a/solution.py
+++ b/solution.py
@@ -56,11 +56,11 @@
 
 def kernel(
     n_energy, n_wire,
-    g_hbm, c_hbm, sl_hbm, sg_hbm, wl_hbm, wg_hbm, pat_hbm, cnt_ref,
-    gl_hbm, gg_hbm, ol_ref, og_ref,
-    g, c, sl, sg, wl, wg, pat,
-    acc, st, pin, lhs, send_w, recv_w, send_g, recv_g, send_s, recv_s,
-    in_sem, out_sem, ring_send, ring_recv, sw_sem, rw_sem, sg_sem, rg_sem, ss_sem, rs_sem,
+    g_hbm, c_hbm, sl_hbm, sg_hbm, wl_hbm, wg_hbm, pat_hbm, cnt_hbm,
+    st, ol_ref, og_ref,
+    g, c, sl, sg, wl, wg, pat, cnt_ref,
+    acc, pin, lhs, send_w, recv_w, send_g, recv_g, send_s, recv_s,
+    in_sem, ring_send, ring_recv, sw_sem, rw_sem, sg_sem, rg_sem, ss_sem, rs_sem,
 ):
     e = lax.axis_index("energy")
     w = lax.axis_index("wire")
@@ -88,7 +88,7 @@
         pl.semaphore_signal(barrier, inc=1, device_id={"wire": w + 1}, device_id_type=MESH)
 
     pairs = [(pat_hbm, pat), (sl_hbm, sl), (sg_hbm, sg), (wl_hbm, wl), (wg_hbm, wg),
-             (g_hbm, g), (c_hbm, c)]
+             (g_hbm, g), (c_hbm, c), (cnt_hbm, cnt_ref)]
     loads = [pltpu.make_async_copy(s, d, in_sem.at[i]) for i, (s, d) in enumerate(pairs)]
     for copy in loads:
         copy.start()
@@ -121,7 +121,7 @@
     lax.fori_loop(1, n_energy, start_w, 0)
     recv_w[e] = send_w[e]
 
-    for i in range(3):
+    for i in (0, 1, 2, 7):
         loads[i].wait()
     chunk = min(slots, 1024)
 
@@ -209,15 +209,6 @@
         for b in range(last):
             advance(b)
 
-    outs = []
-    for b in range(blocks):
-        for k, dst in enumerate((gl_hbm, gg_hbm)):
-            for p in range(2):
-                outs.append(pltpu.make_async_copy(
-                    st.at[b, k, :, pl.ds(p * n, n)], dst.at[p, b], out_sem.at[len(outs)]))
-    for copy in outs:
-        copy.start()
-
     for b in range(blocks):
         for k in range(2):
             hi, lo = split(st[b, k])
@@ -307,7 +298,18 @@
         ring(0).wait_send()
         ring(1).wait_send()
 
-    for copy in outs:
+
+def hand_over(st, ol, og, gl_hbm, gg_hbm, ol_hbm, og_hbm, sem):
+    blocks, n = st.shape[0], st.shape[2]
+    pairs = [(ol, ol_hbm), (og, og_hbm)]
+    for b in range(blocks):
+        for k, dst in enumerate((gl_hbm, gg_hbm)):
+            for p in range(2):
+                pairs.append((st.at[b, k, :, pl.ds(p * n, n)], dst.at[p, b]))
+    copies = [pltpu.make_async_copy(s, d, sem.at[i]) for i, (s, d) in enumerate(pairs)]
+    for copy in copies:
+        copy.start()
+    for copy in copies:
         copy.wait()
 
 
@@ -318,7 +320,6 @@
     rows = 4 * blocks
     g = green_ret.reshape(2, blocks, n, n)
     vals = [x.reshape(2, blocks, slots) for x in (sl, sg, wl, wg)]
-    any_spec = pl.BlockSpec(memory_space=pl.ANY)
     hbm_spec = pl.BlockSpec(memory_space=pltpu.HBM)
     vmem_spec = pl.BlockSpec(memory_space=pltpu.VMEM)
     dma = pltpu.SemaphoreType.DMA
@@ -326,13 +327,12 @@
     out = pl.pallas_call(
         functools.partial(kernel, n_energy, n_wire),
         out_shape=[
-            jax.ShapeDtypeStruct((2, blocks, n, n), F32),
-            jax.ShapeDtypeStruct((2, blocks, n, n), F32),
-            jax.ShapeDtypeStruct((2, blocks, slots), F32),
-            jax.ShapeDtypeStruct((2, blocks, slots), F32),
+            pltpu.VMEM((blocks, 2, n, 2 * n), F32),
+            pltpu.VMEM((2, blocks, slots), F32),
+            pltpu.VMEM((2, blocks, slots), F32),
         ],
-        in_specs=[hbm_spec] * 7 + [pl.BlockSpec(memory_space=pltpu.SMEM)],
-        out_specs=[any_spec, any_spec, vmem_spec, vmem_spec],
+        in_specs=[hbm_spec] * 8,
+        out_specs=[vmem_spec] * 3,
         scratch_shapes=[
             pltpu.VMEM((2, blocks, n, n), F32),
             pltpu.VMEM((2, blocks, n, n), F32),
@@ -341,19 +341,31 @@
             pltpu.VMEM((2, blocks, slots), F32),
             pltpu.VMEM((2, blocks, slots), F32),
             pltpu.VMEM((blocks, slots), jnp.int32),
+            pltpu.SMEM((blocks,), jnp.int32),
             pltpu.VMEM((blocks, n, 8 * n), F32),
-            pltpu.VMEM((blocks, 2, n, 2 * n), F32),
             pltpu.VMEM((2, n, 2 * n), F32),
             pltpu.VMEM((blocks, 4 * n, 2 * n), BF16),
             mail, mail, mail, mail, mail, mail,
-            dma((7,)), dma((4 * blocks,)), dma((2,)), dma((2,)),
+            dma((8,)), dma((2,)), dma((2,)),
             dma((n_energy,)), dma((n_energy,)), dma((n_energy,)),
             dma((n_energy,)), dma((n_energy,)), dma((n_energy,)),
         ],
         compiler_params=pltpu.CompilerParams(
             collective_id=0, has_side_effects=True, vmem_limit_bytes=40 * 1024 * 1024
         ),
-    )(g, coupling, *vals, pattern, counts)
+    )(*[pltpu.with_memory_space_constraint(x, pltpu.HBM) for x in (g, coupling, *vals, pattern, counts)])
+    out = pl.pallas_call(
+        hand_over,
+        out_shape=[
+            jax.ShapeDtypeStruct((2, blocks, n, n), F32),
+            jax.ShapeDtypeStruct((2, blocks, n, n), F32),
+            jax.ShapeDtypeStruct((2, blocks, slots), F32),
+            jax.ShapeDtypeStruct((2, blocks, slots), F32),
+        ],
+        in_specs=[vmem_spec] * 3,
+        out_specs=[hbm_spec] * 4,
+        scratch_shapes=[dma((2 + 4 * blocks,))],
+    )(*[pltpu.with_memory_space_constraint(x, pltpu.VMEM) for x in out])
     return (
         out[0].reshape(green_ret.shape),
         out[1].reshape(green_ret.shape),

time: 44.3 us -> 35 us (0.79)
  local copies, waits for them, and re-layouts: 9.33 us -> 0 us
    unnamed x20 -> x0, local copies, waits for them, and re-layouts: 9.33 us -> none
    pallas_call x1 -> x2, Pallas kernels: 33.9 us -> 34.2 us  [the longest x1 33.3 us: on_device(): pl.pallas_call(functools.partial(kernel, n_energy, n_wire), out_shape=[pl...]
where the time goes in v2:
time: 35 us; the launch traced here: 34.8 us
  Pallas kernels  34.2 us (98%)
  between operations  0.64 us (2%)
    pallas_call x1, Pallas kernels, on_device(): pl.pallas_call(functools.partial(kernel, n_energy, n_wire), out_shape=[pl...  33.3 us
    pallas_call x1, Pallas kernels, on_device(): pl.pallas_call(hand_over, out_shape=[jax.ShapeDtypeStruct((2, blocks, n,...  0.91 us

profile of v2, /device:TPU:3, one launch (start us, length us, event | category | flops | bytes accessed | tf_op | source)
XLA Modules:
  0.0 34.8 jit_solution(15078494707273871686)
XLA Ops:
  0.6 33.3 %shard_map.111 = (f32[2,2,128,256]{3,2,1,0:T(8,128)S(1)}, f32[2,2,4096]{2,1,0:T(2,128)S(1)}, f32[2,2,4096]{2,1,0:T(2,128)S(1)}) custom-call(f32[2,2,128,128]{3,2,1,0:T(8,128)} %bitcast.17, f32[2,2,128,128]{3,2,1,0:T(8,128)} %c_hbm.1, f32[2,2,4096]{2,1,0:T(2,128)} %bitcast.18, f32[2,2,4096]{2,1,0:T(2,128)} %bitcast.19, f32[2,2,4096]{2,1,0:T(2,128)} %bitcast.20, ...), custom_call_target="tpu_custom_call" | custom-call | tf_op jit(solution)/shard_map/pallas_call | solution.py:327
  33.9 0.9 %shard_map.112 = (f32[2,2,128,128]{3,2,1,0:T(8,128)}, f32[2,2,128,128]{3,2,1,0:T(8,128)}, f32[2,2,4096]{2,1,0:T(2,128)}, f32[2,2,4096]{2,1,0:T(2,128)}) custom-call(f32[2,2,128,256]{3,2,1,0:T(8,128)S(1)} %get-tuple-element.11.st, f32[2,2,4096]{2,1,0:T(2,128)S(1)} %get-tuple-element.12.ol, f32[2,2,4096]{2,1,0:T(2,128)S(1)} %get-tuple-element.13.og), custom_call_target="tpu_custom_call" | custom-call | tf_op jit(solution)/shard_map/pallas_call | solution.py:357

commit v3 on v2

--- a/solution.py
+++ b/solution.py
@@ -16,6 +16,11 @@
     hi = x.astype(BF16)
     lo = (x - hi.astype(F32)).astype(BF16)
     return hi, lo
+
+
+def down_rows(row, n):
+    tile = jnp.broadcast_to(row, (16, row.shape[1])).astype(BF16)
+    return jnp.concatenate([tile] * (n // 16), axis=0)
 
 
 def dot_nn(a, b):
@@ -52,6 +57,12 @@
     )
     out = dot3(dot_nn, row, wide)
     return out[:, : 2 * n], out[:, 2 * n :]
+
+
+def sandwich_one(row, square, state):
+    n = row[0].shape[0]
+    right = split(dot3(dot_nt, split(state), square))
+    return dot3(dot_nn, row, full(right))
 
 
 def kernel(
@@ -93,37 +104,9 @@
     for copy in loads:
         copy.start()
 
-    loads[3].wait()
-    loads[4].wait()
-    for t in range(n_energy):
-        for p in range(2):
-            for k, ref in enumerate((wl, wg)):
-                for b in range(blocks):
-                    row = p * 2 * blocks + k * blocks + b
-                    send_w[t, row : row + 1, :] = ref[p, b : b + 1, t * part : (t + 1) * part]
-    beside = jnp.where(w > 0, 1, 0) + jnp.where(w < n_wire - 1, 1, 0)
-    pl.semaphore_wait(barrier, n_energy - 1 + beside)
-
-    def to_peer(src, dst, s_sem, r_sem, peer):
-        return pltpu.make_async_remote_copy(
-            src_ref=src.at[peer], dst_ref=dst.at[e], send_sem=s_sem.at[peer],
-            recv_sem=r_sem.at[e], device_id={"energy": peer}, device_id_type=MESH)
-
-    def from_peer(src, dst, s_sem, r_sem, peer):
-        return pltpu.make_async_remote_copy(
-            src_ref=src.at[peer], dst_ref=dst.at[peer], send_sem=s_sem.at[peer],
-            recv_sem=r_sem.at[peer], device_id={"energy": peer}, device_id_type=MESH)
-
-    def start_w(d, carry):
-        to_peer(send_w, recv_w, sw_sem, rw_sem, lax.rem(e + d, n_energy)).start()
-        return carry
-
-    lax.fori_loop(1, n_energy, start_w, 0)
-    recv_w[e] = send_w[e]
-
     for i in (0, 1, 2, 7):
         loads[i].wait()
-    chunk = min(slots, 1024)
+    chunk = min(slots, 2048)
 
     def places(b, off, size):
         p = pat[b : b + 1, pl.ds(off, size)]
@@ -139,15 +122,16 @@
         off = pl.multiple_of(i * chunk, chunk)
         for b in range(blocks):
             row_is, col_is = places(b, off, chunk)
-            hot = jnp.where(row_is, 1.0, 0.0).astype(BF16)
+            hot = jnp.where(col_is, 1.0, 0.0).astype(BF16)
+            row_hot = jnp.where(row_is, 1.0, 0.0).astype(BF16)
             his, los = [], []
             for ref in (sl, sg):
                 for p in range(2):
                     v = ref[p, b : b + 1, pl.ds(off, chunk)]
                     hi = v.astype(BF16).astype(F32)
-                    his.append(jnp.where(col_is, hi, 0.0).astype(BF16))
-                    los.append(jnp.where(col_is, v - hi, 0.0).astype(BF16))
-            acc[b] += dot_nt(hot, jnp.concatenate(his + los, axis=0))
+                    his.append(row_hot * down_rows(hi, n))
+                    los.append(row_hot * down_rows(v - hi, n))
+            acc[b] += dot_nt(jnp.concatenate(his + los, axis=0), hot)
         return carry
 
     lax.fori_loop(0, slots // chunk, scatter, 0)
@@ -162,8 +146,10 @@
         c_row = split(jnp.concatenate([c[0, b], c[1, b]], axis=1))
         mult = split(dot3(dot_nn, g_row, full(c_row)))
         dense = acc[b]
-        dense = dense[:, : 4 * n] + dense[:, 4 * n :]
-        source = sandwich(g_row, full(g_row), jnp.stack([dense[:, : 2 * n], dense[:, 2 * n :]]))
+        dense = dense[: 4 * n] + dense[4 * n :]
+        less = jnp.concatenate([dense[:n], dense[n : 2 * n]], axis=1)
+        greater = jnp.concatenate([dense[2 * n : 3 * n], dense[3 * n :]], axis=1)
+        source = sandwich(g_row, full(g_row), jnp.stack([less, greater]))
         if b == 0:
             through = mult
             total = source
@@ -176,6 +162,31 @@
         st[b, 1] = total[1]
         mults.append(through)
 
+    loads[3].wait()
+    loads[4].wait()
+    for t in range(n_energy):
+        for p in range(2):
+            for k, ref in enumerate((wl, wg)):
+                for b in range(blocks):
+                    row = p * 2 * blocks + k * blocks + b
+                    send_w[t, row : row + 1, :] = ref[p, b : b + 1, t * part : (t + 1) * part]
+    beside = jnp.where(w > 0, 1, 0) + jnp.where(w < n_wire - 1, 1, 0)
+    pl.semaphore_wait(barrier, n_energy - 1 + beside)
+
+    def to_peer(src, dst, s_sem, r_sem, peer):
+        return pltpu.make_async_remote_copy(
+            src_ref=src.at[peer], dst_ref=dst.at[e], send_sem=s_sem.at[peer],
+            recv_sem=r_sem.at[e], device_id={"energy": peer}, device_id_type=MESH)
+
+    def from_peer(src, dst, s_sem, r_sem, peer):
+        return pltpu.make_async_remote_copy(
+            src_ref=src.at[peer], dst_ref=dst.at[peer], send_sem=s_sem.at[peer],
+            recv_sem=r_sem.at[peer], device_id={"energy": peer}, device_id_type=MESH)
+
+    def start_w(d, carry):
+        to_peer(send_w, recv_w, sw_sem, rw_sem, lax.rem(e + d, n_energy)).start()
+        return carry
+
     last = blocks - 1
 
     def ring(k):
@@ -188,26 +199,32 @@
             src_ref=st.at[last, k], dst_ref=pin.at[k], send_sem=ring_send.at[k],
             recv_sem=ring_recv.at[k], device_id={"wire": w - 1}, device_id_type=MESH)
 
-    def advance(b):
-        more = sandwich(mults[b], full(mults[b]), pin[...])
-        st[b, 0] += more[0]
-        st[b, 1] += more[1]
-
-    @pl.when(w > 0)
+    def advance(b, k):
+        st[b, k] += sandwich_one(mults[b], full(mults[b]), pin[k])
+
+    @pl.when(w == 0)
     def _():
-        arrive(0).wait_recv()
-        arrive(1).wait_recv()
-        advance(last)
-
-    @pl.when(w < n_wire - 1)
-    def _():
-        ring(0).start()
-        ring(1).start()
+        for k in range(2):
+            ring(k).start()
+
+    lax.fori_loop(1, n_energy, start_w, 0)
+    recv_w[e] = send_w[e]
+    for k in range(2):
+
+        @pl.when(w > 0)
+        def _():
+            arrive(k).wait_recv()
+            advance(last, k)
+
+        @pl.when(jnp.logical_and(w > 0, w < n_wire - 1))
+        def _():
+            ring(k).start()
 
     @pl.when(w > 0)
     def _():
         for b in range(last):
-            advance(b)
+            for k in range(2):
+                advance(b, k)
 
     for b in range(blocks):
         for k in range(2):
@@ -342,7 +359,7 @@
             pltpu.VMEM((2, blocks, slots), F32),
             pltpu.VMEM((blocks, slots), jnp.int32),
             pltpu.SMEM((blocks,), jnp.int32),
-            pltpu.VMEM((blocks, n, 8 * n), F32),
+            pltpu.VMEM((blocks, 8 * n, n), F32),
             pltpu.VMEM((2, n, 2 * n), F32),
             pltpu.VMEM((blocks, 4 * n, 2 * n), BF16),
             mail, mail, mail, mail, mail, mail,

time: 35 us -> 30.7 us (0.88)
  Pallas kernels: 34.2 us -> 29.9 us
    pallas_call x1, Pallas kernels: 33.3 us -> 29 us  [on_device(): pl.pallas_call(functools.partial(kernel, n_energy, n_wire), out_shape=[pl...]
where the time goes in v3:
time: 30.7 us; the launch traced here: 30.6 us
  Pallas kernels  29.9 us (97%)
  between operations  0.64 us (2%)
    pallas_call x1, Pallas kernels, on_device(): pl.pallas_call(functools.partial(kernel, n_energy, n_wire), out_shape=[pl...  29 us
    pallas_call x1, Pallas kernels, on_device(): pl.pallas_call(hand_over, out_shape=[jax.ShapeDtypeStruct((2, blocks, n,...  0.91 us

profile of v3, /device:TPU:3, one launch (start us, length us, event | category | flops | bytes accessed | tf_op | source)
XLA Modules:
  0.0 30.6 jit_solution(6546680068424093721)
XLA Ops:
  0.6 29.0 %shard_map.111 = (f32[2,2,128,256]{3,2,1,0:T(8,128)S(1)}, f32[2,2,4096]{2,1,0:T(2,128)S(1)}, f32[2,2,4096]{2,1,0:T(2,128)S(1)}) custom-call(f32[2,2,128,128]{3,2,1,0:T(8,128)} %bitcast.17, f32[2,2,128,128]{3,2,1,0:T(8,128)} %c_hbm.1, f32[2,2,4096]{2,1,0:T(2,128)} %bitcast.18, f32[2,2,4096]{2,1,0:T(2,128)} %bitcast.19, f32[2,2,4096]{2,1,0:T(2,128)} %bitcast.20, ...), custom_call_target="tpu_custom_call" | custom-call | tf_op jit(solution)/shard_map/pallas_call | solution.py:344
  29.7 0.9 %shard_map.112 = (f32[2,2,128,128]{3,2,1,0:T(8,128)}, f32[2,2,128,128]{3,2,1,0:T(8,128)}, f32[2,2,4096]{2,1,0:T(2,128)}, f32[2,2,4096]{2,1,0:T(2,128)}) custom-call(f32[2,2,128,256]{3,2,1,0:T(8,128)S(1)} %get-tuple-element.11.st, f32[2,2,4096]{2,1,0:T(2,128)S(1)} %get-tuple-element.12.ol, f32[2,2,4096]{2,1,0:T(2,128)S(1)} %get-tuple-element.13.og), custom_call_target="tpu_custom_call" | custom-call | tf_op jit(solution)/shard_map/pallas_call | solution.py:374

commit v4 on v3

--- a/solution.py
+++ b/solution.py
@@ -173,6 +173,13 @@
     beside = jnp.where(w > 0, 1, 0) + jnp.where(w < n_wire - 1, 1, 0)
     pl.semaphore_wait(barrier, n_energy - 1 + beside)
 
+    middle = n_energy // 2
+
+    def far(d):
+        if n_energy % 2:
+            return d
+        return jnp.where(d <= middle, d + middle - 1, d - middle)
+
     def to_peer(src, dst, s_sem, r_sem, peer):
         return pltpu.make_async_remote_copy(
             src_ref=src.at[peer], dst_ref=dst.at[e], send_sem=s_sem.at[peer],
@@ -235,7 +242,7 @@
                 lhs[b, at : at + n, n:] = lo[:, p * n : (p + 1) * n]
 
     def gather(d, carry):
-        t = lax.rem(e + d, n_energy)
+        t = lax.rem(e + jnp.where(d < n_energy, far(d), 0), n_energy)
         off = pl.multiple_of(t * part, part)
         for b in range(blocks):
             row_is, col_is = places(b, off, part)
@@ -282,10 +289,11 @@
             total = term if total is None else total + term
         send_s[f] = jnp.concatenate([-scale * total[half:], scale * total[:half]], axis=0)
 
-        @pl.when(e != f)
-        def _():
-            to_peer(send_s, recv_s, ss_sem, rs_sem, f).start()
-
+    def start_s(d, carry):
+        to_peer(send_s, recv_s, ss_sem, rs_sem, lax.rem(e + far(d), n_energy)).start()
+        return carry
+
+    lax.fori_loop(1, n_energy, start_s, 0)
     recv_s[e] = send_s[e]
 
     def land_s(d, carry):

time: 30.7 us -> 31.4 us (1.023)
  Pallas kernels: 29.9 us -> 30.4 us
    pallas_call x1, Pallas kernels: 29 us -> 29.5 us  [on_device(): pl.pallas_call(functools.partial(kernel, n_energy, n_wire), out_shape=[pl...]
where the time goes in v4:
time: 31.4 us; the launch traced here: 31.1 us
  Pallas kernels  30.4 us (97%)
  between operations  0.64 us (2%)
    pallas_call x1, Pallas kernels, on_device(): pl.pallas_call(functools.partial(kernel, n_energy, n_wire), out_shape=[pl...  29.5 us
    pallas_call x1, Pallas kernels, on_device(): pl.pallas_call(hand_over, out_shape=[jax.ShapeDtypeStruct((2, blocks, n,...  0.91 us

profile of v4, /device:TPU:3, one launch (start us, length us, event | category | flops | bytes accessed | tf_op | source)
XLA Modules:
  0.0 31.1 jit_solution(2567522958570767126)
XLA Ops:
  0.6 29.5 %shard_map.111 = (f32[2,2,128,256]{3,2,1,0:T(8,128)S(1)}, f32[2,2,4096]{2,1,0:T(2,128)S(1)}, f32[2,2,4096]{2,1,0:T(2,128)S(1)}) custom-call(f32[2,2,128,128]{3,2,1,0:T(8,128)} %bitcast.17, f32[2,2,128,128]{3,2,1,0:T(8,128)} %c_hbm.1, f32[2,2,4096]{2,1,0:T(2,128)} %bitcast.18, f32[2,2,4096]{2,1,0:T(2,128)} %bitcast.19, f32[2,2,4096]{2,1,0:T(2,128)} %bitcast.20, ...), custom_call_target="tpu_custom_call" | custom-call | tf_op jit(solution)/shard_map/pallas_call | solution.py:352
  30.2 0.9 %shard_map.112 = (f32[2,2,128,128]{3,2,1,0:T(8,128)}, f32[2,2,128,128]{3,2,1,0:T(8,128)}, f32[2,2,4096]{2,1,0:T(2,128)}, f32[2,2,4096]{2,1,0:T(2,128)}) custom-call(f32[2,2,128,256]{3,2,1,0:T(8,128)S(1)} %get-tuple-element.11.st, f32[2,2,4096]{2,1,0:T(2,128)S(1)} %get-tuple-element.12.ol, f32[2,2,4096]{2,1,0:T(2,128)S(1)} %get-tuple-element.13.og), custom_call_target="tpu_custom_call" | custom-call | tf_op jit(solution)/shard_map/pallas_call | solution.py:382
